TPU v7x, 32 devices: a whole 2x2x4 slice. The times are simulated.
32 devices in a mesh: seg: 8 (over z, x), space: 4 (over y, core).
Axes of the slice: x: 2, y: 2, z: 4, core: 2. Of those that a mesh axis runs over, the one named last changes fastest.
Arguments:
- states: float32 [8, 32, 65, 128], P('seg', 'space'), may hold values from -6 to 6
- forcing: float32 [32, 65, 128], P('space'), may hold values from -6 to 6
- wall_viscosity: float32 [65], replicated, may hold values from 0.5 to 4
Outputs:
- new_states: float32 [8, 32, 65, 128], P('seg', 'space')
- mismatch: float32 [8, 32, 65, 128], P('seg', 'space')
All inputs are finite; a program needn't handle non-finite values.
Results may differ from a plain program's by a relative error of at most 0.0075.
Values sent between devices are 32-bit elements; how exact they have to be, the bound alone decides.
No kernel may reach another device: no remote copies, remote signals or barrier semaphores. Data moves between devices by JAX's collectives and lax.ppermute only.
A program may use at most 64 MiB of HBM per device.

v0:
```python
import jax
import jax.numpy as jnp
from jax import lax
from jax.sharding import PartitionSpec as P

NY = 65
STEPS = 4
ITERS = 2
ADVECT = 0.15
SPREAD = 0.2
PUSHED = 0.25
EPSILON = 1e-06


def padded_2(shard, sides, width):
    for axis, dim in sides:
        devices, length = (lax.axis_size(axis), shard.shape[dim])
        up = [(i, (i + 1) % devices) for i in range(devices)]
        down = [(j, i) for i, j in up]
        last = lax.slice_in_dim(shard, length - width, length, axis=dim)
        initial = lax.slice_in_dim(shard, 0, width, axis=dim)
        before = lax.ppermute(last, axis, up)
        after = lax.ppermute(initial, axis, down)
        shard = jnp.concatenate([before, shard, after], axis=dim)
    return shard


def shifted(block, axis, distance):
    devices = range(lax.axis_size(axis))
    route = [((i - distance) % len(devices), i) for i in devices]
    return lax.ppermute(block, axis, route)


def inverses(viscosity):
    points = viscosity.shape[0]
    zero = jnp.zeros((1,), jnp.float32)
    negative = -viscosity
    centre = 1.0 + 2.0 * viscosity
    lower = jnp.concatenate([zero, negative[1:]])
    upper = jnp.concatenate([negative[:-1], zero])
    identity = jnp.eye(points, dtype=jnp.float32)
    return lax.linalg.tridiagonal_solve(lower[None], centre[None], upper[None], identity[None])[0]


def apply_inverse(inverse, field):
    return jnp.einsum("jk,xkz->xjz", inverse, field, precision=lax.Precision.HIGHEST)


def apply_transposed(inverse, field):
    return jnp.einsum("kj,xkz->xjz", inverse, field, precision=lax.Precision.HIGHEST)


def spanwise(field):
    return jnp.roll(field, 1, 2) + jnp.roll(field, -1, 2) - 2.0 * field


def forward_step(field, forcing, base, inverse):
    padded = padded_2(field, (("space", 0),), 1)
    slope = 0.5 * (padded[2:] - padded[:-2])
    pushed = field - ADVECT * (base + field) * slope + SPREAD * spanwise(field) + PUSHED * forcing
    return (apply_inverse(inverse, pushed), slope)


def adjoint_step(weight, field, slope, base, inverse):
    carried = apply_transposed(inverse, weight)
    flux = (base + field) * carried
    padded = padded_2(flux, (("space", 0),), 1)
    return (
        carried
        - ADVECT * carried * slope
        + ADVECT * (0.5 * (padded[2:] - padded[:-2]))
        + SPREAD * spanwise(carried)
    )


def integrate(field, forcing, base, inverse):
    saved = []
    for step in range(STEPS):
        following, slope = forward_step(field, forcing, base, inverse)
        saved.append((field, slope))
        field = following
    return (field, saved)


def adjoint(weight, saved, base, inverse):
    for step in reversed(range(len(saved))):
        weight = adjoint_step(weight, saved[step][0], saved[step][1], base, inverse)
    return weight


def per_device(states, forcing, wall_viscosity):
    current = states[0]
    base = (2.0 * jnp.arange(NY, dtype=jnp.float32) / (NY - 1) - 1.0)[None, :, None]
    inverse = inverses(wall_viscosity)
    mismatch = current
    for iteration in range(ITERS):
        ending, saved = integrate(current, forcing, base, inverse)
        prior = shifted(ending, "seg", 1)
        earlier = prior - current
        mismatch = shifted(earlier, "seg", -1)
        back = adjoint(mismatch, saved, base, inverse)
        descent = back - earlier
        total, squares = lax.psum(
            (0.5 * jnp.sum(mismatch * mismatch), jnp.sum(descent * descent)), ("seg", "space")
        )
        current = current - total / (squares + EPSILON) * descent
    return (current[None], mismatch[None])


def solution(mesh):
    placed = (P("seg", "space", None, None), P("space", None, None), P())
    return jax.shard_map(
        per_device,
        mesh=mesh,
        in_specs=placed,
        out_specs=(P("seg", "space", None, None), P("seg", "space", None, None)),
        check_vma=False,
    )
```

profile of v0, /device:TPU:0, one launch (start us, length us, event | category | flops | bytes accessed | tf_op | source)
XLA Modules:
  0.0 419.8 jit_solution(12235927826151954652)
XLA Ops:
  0.6 1.0 copy.69
  1.7 2.5 collective-permute-start
  5.8 170.1 %while.32 = (s32[]{:T(128)}, f32[1]{0:T(128)}, f32[1,65]{1,0:T(1,128)S(1)}, f32[2,32,1]{1,2,0:T(1,128)S(1)}, f32[2,32,1,65]{3,1,2,0:T(8,128)S(1)}, /*index=5*/f3...) while((s32[]{:T(128)}, f32[1]{0:T(128)}, ...), condition=%wide.region_1.2_spmd, body=%wide.region_0.1_spmd.sunk | while | flops 6369 | bytes 103045 | solution.py:42
  7.9 0.7 fusion.724
  8.6 0.7 fusion.726
  10.0 0.7 fusion.725
  73.4 0.7 constant_dynamic-update-slice_fusion.140
  92.9 0.7 fusion.724
  93.6 0.7 fusion.726
  95.1 0.7 fusion.725
  175.8 44.2 %while.33 = (s32[]{:T(128)}, f32[1,65]{1,0:T(1,128)S(1)}, f32[2,32,1,65]{3,1,2,0:T(8,128)S(1)}, f32[2,32,1,65]{3,2,1,0:T(1,128)S(1)}, f32[2,32,1]{1,2,0:T(1,128)...) while((s32[]{:T(128)}, f32[1,65]{1,0:T(1,128)S(1)}, ...), condition=%wide.region_3.4_spmd, body=%wide.region_2.3_spmd.sunk | while | flops 4193 | bytes 91485 | solution.py:42
  176.6 0.7 fusion.729
  177.3 19.5 %constant_dynamic-update-slice_fusion.168 = (f32[32,1,65]{2,1,0:T(1,128)S(1)}, f32[1,65]{1,0:T(1,128)S(1)}, f32[1,65]{1,0:T(1,128)S(1)}, f32[1,65]{1,0:T(1,128)S...) fusion(f32[]{:T(128)} %bitcast.1400, ...), kind=kLoop, calls=%fused_computation.196.clone.1 | loop fusion | flops 4029 | bytes 24956 | tf_op jit(solution)/shard_map/vmap()/while
  198.7 0.7 fusion.729
  199.4 19.5 %constant_dynamic-update-slice_fusion.168 = (f32[32,1,65]{2,1,0:T(1,128)S(1)}, f32[1,65]{1,0:T(1,128)S(1)}, f32[1,65]{1,0:T(1,128)S(1)}, f32[1,65]{1,0:T(1,128)S...) fusion(f32[]{:T(128)} %bitcast.1400, ...), kind=kLoop, calls=%fused_computation.196.clone.1 | loop fusion | flops 4029 | bytes 24956 | tf_op jit(solution)/shard_map/vmap()/while
  221.0 1.8 collective-permute-start.2
  222.9 1.7 collective-permute-done.2
  224.6 1.6 collective-permute-done.3
  227.9 1.5 collective-permute-done.4
  229.4 1.7 collective-permute-done.5
  232.7 1.3 collective-permute-done.6
  234.0 1.9 collective-permute-done.7
  235.8 1.5 convolution_bitcast_fusion.12
  237.3 1.6 collective-permute-start.8
  238.9 8.8 %collective-permute-done.8 = f32[8,65,128]{2,1,0:T(8,128)S(1)} collective-permute-done((f32[8,65,128]{2,1,0:T(8,128)S(1)}, f32[8,65,128]{2,1,0:T(8,128)S(1)}, u32[]{:S(2)}, u32[]{:S(2)}) %collective-permute-start.8) | collective-permute-done | bytes 266272 | tf_op jit(solution)/shard_map/ppermute | solution.py:31
  247.8 1.8 collective-permute-start.9
  249.6 5.0 %collective-permute-done.9 = f32[8,65,128]{2,1,0:T(8,128)S(1)} collective-permute-done((f32[8,65,128]{2,1,0:T(8,128)S(1)}, f32[8,65,128]{2,1,0:T(8,128)S(1)}, u32[]{:S(2)}, u32[]{:S(2)}) %collective-permute-start.9) | collective-permute-done | bytes 266272 | tf_op jit(solution)/shard_map/ppermute | solution.py:31
  255.2 0.9 fusion.694
  256.7 1.6 collective-permute-start.10
  259.5 0.8 collective-permute-done.10
  260.3 2.3 collective-permute-done.11
  262.5 1.7 add_multiply_fusion.5
  265.1 0.8 collective-permute-done.12
  266.0 2.0 collective-permute-done.13
  269.5 0.8 collective-permute-done.14
  270.3 2.0 collective-permute-done.15
  273.8 0.8 collective-permute-done.16
  274.7 2.0 collective-permute-done.17
  276.6 0.9 multiply_reduce_fusion.2
  277.5 40.1 %all-reduce.1 = (f32[]{:T(128)}, f32[]{:T(128)}) all-reduce(f32[]{:T(128)S(6)} %mul.1494, f32[]{:T(128)} %get-tuple-element.304), channel_id=1, replica_groups=mesh['seg'=8,'space'=4] {'seg','space'}, use_global_device_ids=true, to_apply=%region_5.6 | all-reduce | flops 2 | bytes 16 | tf_op jit(solution)/shard_map/psum | solution.py:103
  319.9 1.1 collective-permute-done.18
  321.0 2.7 collective-permute-done.19
  325.2 1.0 collective-permute-done.20
  326.2 2.0 collective-permute-done.21
  329.7 1.0 collective-permute-done.22
  330.7 2.0 collective-permute-done.23
  334.2 1.0 collective-permute-done.24
  335.2 2.0 collective-permute-done.25
  337.9 1.9 collective-permute-start.26
  339.8 9.8 %collective-permute-done.26 = f32[8,65,128]{2,1,0:T(8,128)S(1)} collective-permute-done((f32[8,65,128]{2,1,0:T(8,128)S(1)}, f32[8,65,128]{2,1,0:T(8,128)S(1)}, u32[]{:S(2)}, u32[]{:S(2)}) %collective-permute-start.26) | collective-permute-done | bytes 266272 | tf_op jit(solution)/shard_map/ppermute | solution.py:31
  349.8 8.2 %collective-permute-done.27 = f32[8,65,128]{2,1,0:T(8,128)S(1)} collective-permute-done((f32[8,65,128]{2,1,0:T(8,128)S(1)}, f32[8,65,128]{2,1,0:T(8,128)S(1)}, u32[]{:S(2)}, u32[]{:S(2)}) %collective-permute-start.27) | collective-permute-done | bytes 266272 | tf_op jit(solution)/shard_map/ppermute | solution.py:31
  358.5 0.9 fusion.670
  361.9 0.8 copy.22
  362.7 1.1 collective-permute-done.29
  363.7 1.4 add_multiply_fusion.1
  366.1 1.2 collective-permute-done.30
  367.3 1.7 collective-permute-done.31
  370.5 1.1 collective-permute-done.32
  371.6 1.7 collective-permute-done.33
  374.9 1.1 collective-permute-done.34
  376.0 1.7 collective-permute-done.35
  377.7 0.9 multiply_reduce_fusion
  378.6 39.1 %all-reduce = (f32[]{:T(128)}, f32[]{:T(128)}) all-reduce(f32[]{:T(128)S(6)} %mul.1544, f32[]{:T(128)} %get-tuple-element.302), channel_id=1, replica_groups=mesh['seg'=8,'space'=4] {'seg','space'}, use_global_device_ids=true, to_apply=%region_9.10 | all-reduce | flops 2 | bytes 16 | tf_op jit(solution)/shard_map/psum | solution.py:103
  419.0 0.8 copy.21
  (301 shorter events, 72.5 us)
Async XLA Ops:
  1.7 218.4 %collective-permute-start = (f32[1,65,128]{2,1,0:T(8,128)S(1)}, f32[1,65,128]{2,1,0:T(8,128)S(1)}, u32[]{:S(2)}, u32[]{:S(2)}) collective-permute-start(f32[1,65,128]{2,1,0:T(8,128)S(1)} %get-tuple-element.526), channel_id=1, source_target_pairs={{1,0},{2,1},{3,2},{0,3},{5,4},{6,5},{7,6},{4,7},{9,8},{10,9},{11,1... | collective-permute-start | bytes 99848 | tf_op jit(solution)/shard_map/ppermute | solution.py:23
  4.1 216.0 %collective-permute-start.1 = (f32[1,65,128]{2,1,0:T(8,128)S(1)}, f32[1,65,128]{2,1,0:T(8,128)S(1)}, u32[]{:S(2)}, u32[]{:S(2)}) collective-permute-start(f32[1,65,128]{2,1,0:T(8,128)S(1)} %get-tuple-element.527), channel_id=1, source_target_pairs={{0,1},{1,2},{2,3},{3,0},{4,5},{5,6},{6,7},{7,4},{8,9},{9,10},{10,1... | collective-permute-start | bytes 99848 | tf_op jit(solution)/shard_map/ppermute | solution.py:22
  4.3 0.7 copy-start.17
  175.8 44.3 %copy-start = (f32[8,65,128]{2,0,1:T(8,128)S(1)}, f32[8,65,128]{2,0,1:T(8,128)}, u32[]{:S(2)}) copy-start(f32[8,65,128]{2,0,1:T(8,128)} %param.8) | copy-start | bytes 798724
  220.1 0.7 copy-start.3
  220.1 0.7 copy-start.5
  221.0 3.6 collective-permute-start.2
  222.8 3.4 collective-permute-start.3
  224.6 2.3 copy-start.7
  226.1 0.7 copy-start.9
  227.0 2.4 collective-permute-start.4
  227.7 3.4 collective-permute-start.5
  229.4 2.4 copy-start.11
  231.1 0.7 copy-start.13
  232.0 2.0 collective-permute-start.6
  232.3 3.5 collective-permute-start.7
  235.8 11.9 %copy-start.1 = (f32[1,8,65,128]{3,1,2,0:T(8,128)S(1)}, f32[1,8,65,128]{3,1,2,0:T(8,128)}, u32[]{:S(2)}) copy-start(f32[1,8,65,128]{3,1,2,0:T(8,128)} %param.7) | copy-start | bytes 798724
  237.3 10.4 %collective-permute-start.8 = (f32[8,65,128]{2,1,0:T(8,128)S(1)}, f32[8,65,128]{2,1,0:T(8,128)S(1)}, u32[]{:S(2)}, u32[]{:S(2)}) collective-permute-start(f32[8,65,128]{2,1,0:T(8,128)S(1)} %convolution_bitcast_fusion.12), channel_id=1, source_target_pairs={{28,0},{0,4},{4,8},{8,12},{12,16},{16,20},{20,24},{24,28},{29,1},{... | collective-permute-start | bytes 798728 | tf_op jit(solution)/shard_map/ppermute | solution.py:31
  247.8 6.8 %collective-permute-start.9 = (f32[8,65,128]{2,1,0:T(8,128)S(1)}, f32[8,65,128]{2,1,0:T(8,128)S(1)}, u32[]{:S(2)}, u32[]{:S(2)}) collective-permute-start(f32[8,65,128]{2,1,0:T(8,128)S(1)} %bitcast_subtract_fusion), channel_id=1, source_target_pairs={{4,0},{8,4},{12,8},{16,12},{20,16},{24,20},{28,24},{0,28},{5,1},{9... | collective-permute-start | bytes 798728 | tf_op jit(solution)/shard_map/ppermute | solution.py:31
  256.7 3.6 collective-permute-start.10
  258.3 4.2 %collective-permute-start.11 = (f32[1,65,128]{2,1,0:T(8,128)}, f32[1,65,128]{2,1,0:T(8,128)}, u32[]{:S(2)}, u32[]{:S(2)}) collective-permute-start(f32[1,65,128]{2,1,0:T(8,128)} %get-tuple-element.507), channel_id=1, source_target_pairs={{0,1},{1,2},{2,3},{3,0},{4,5},{5,6},{6,7},{7,4},{8,9},{9,10},{10,1... | collective-permute-start | bytes 99848 | tf_op jit(solution)/shard_map/ppermute | solution.py:22
  264.3 1.7 collective-permute-start.12
  264.3 3.6 collective-permute-start.13
  265.0 3.0 copy-start.12
  265.0 2.9 copy-start.14
  268.6 1.7 collective-permute-start.14
  268.7 3.6 collective-permute-start.15
  269.3 2.9 copy-start.8
  269.3 2.9 copy-start.10
  273.0 1.7 collective-permute-start.16
  273.0 3.6 collective-permute-start.17
  273.7 2.9 copy-start.4
  273.7 2.9 copy-start.6
  319.2 1.8 collective-permute-start.18
  319.4 4.3 %collective-permute-start.19 = (f32[1,65,128]{2,1,0:T(8,128)S(1)}, f32[1,65,128]{2,1,0:T(8,128)S(1)}, u32[]{:S(2)}, u32[]{:S(2)}) collective-permute-start(f32[1,65,128]{2,1,0:T(8,128)S(1)} %get-tuple-element.479), channel_id=1, source_target_pairs={{0,1},{1,2},{2,3},{3,0},{4,5},{5,6},{6,7},{7,4},{8,9},{9,10},{10,1... | collective-permute-start | bytes 99848 | tf_op jit(solution)/shard_map/ppermute | solution.py:22
  324.5 1.7 collective-permute-start.20
  324.6 3.6 collective-permute-start.21
  329.0 1.7 collective-permute-start.22
  329.1 3.6 collective-permute-start.23
  333.5 1.7 collective-permute-start.24
  333.6 3.6 collective-permute-start.25
  337.2 0.7 copy-start.15
  337.9 11.8 %collective-permute-start.26 = (f32[8,65,128]{2,1,0:T(8,128)S(1)}, f32[8,65,128]{2,1,0:T(8,128)S(1)}, u32[]{:S(2)}, u32[]{:S(2)}) collective-permute-start(f32[8,65,128]{2,1,0:T(8,128)S(1)} %convolution_bitcast_fusion.4), channel_id=1, source_target_pairs={{28,0},{0,4},{4,8},{8,12},{12,16},{16,20},{20,24},{24,28},{29,1},{... | collective-permute-start | bytes 798728 | tf_op jit(solution)/shard_map/ppermute | solution.py:31
  349.7 8.2 %collective-permute-start.27 = (f32[8,65,128]{2,1,0:T(8,128)S(1)}, f32[8,65,128]{2,1,0:T(8,128)S(1)}, u32[]{:S(2)}, u32[]{:S(2)}) collective-permute-start(f32[8,65,128]{2,1,0:T(8,128)S(1)} %sub.738), channel_id=1, source_target_pairs={{4,0},{8,4},{12,8},{16,12},{20,16},{24,20},{28,24},{0,28},{5,1},{9... | collective-permute-start | bytes 798728 | tf_op jit(solution)/shard_map/ppermute | solution.py:31
  360.0 2.6 collective-permute-start.28
  360.0 3.7 collective-permute-start.29
  361.9 1.9 copy-start.2
  361.9 1.9 copy-start.16
  365.2 2.1 collective-permute-start.30
  365.6 3.4 collective-permute-start.31
  369.6 2.0 collective-permute-start.32
  370.0 3.4 collective-permute-start.33
  374.1 1.9 collective-permute-start.34
  374.3 3.4 collective-permute-start.35
where the time goes:
time: 423 us; the launch traced here: 420 us
  loops' own time  120 us (28%)
  other arithmetic  85.2 us (20%)
  blocking collectives  79.3 us (19%)
  waiting for transfers between devices  75.2 us (18%)
  local copies, waits for them, and re-layouts  23.4 us (6%)
  starting transfers between devices  18.6 us (4%)
  matrix products  12.9 us (3%)
  between operations  5.19 us (1%)
    another operation x2, loops' own time, inverses(): lax.linalg.tridiagonal_solve(lower[None], centre[None], upper[None], iden...  120 us
    psum x2, blocking collectives, per_device(): lax.psum((0.5 * jnp.sum(mismatch * mismatch), jnp.sum(descent * descent))...  79.3 us
    while x62, other arithmetic  77.8 us
    ppermute x4, waiting for transfers between devices, shifted(): return lax.ppermute(block, axis, route)  31.9 us
    ppermute x16, waiting for transfers between devices, padded_2(): before = lax.ppermute(last, axis, up)  28.1 us
    ppermute x16, waiting for transfers between devices, padded_2(): after = lax.ppermute(initial, axis, down)  15.2 us
    slice x20, local copies, waits for them, and re-layouts, inverses(): lax.linalg.tridiagonal_solve(lower[None], centre[None], upper[None], iden...  11.7 us
    ppermute x16, starting transfers between devices, padded_2(): after = lax.ppermute(initial, axis, down)  8.5 us
  transfers between devices with their start and end apart: 36, of which 33 were waited for; matrix products, arithmetic and copies ran while one was open for 24% of the time, Pallas kernels for 0%

commit v1 on v0

--- a/solution.py
+++ b/solution.py
@@ -101,7 +101,8 @@
         back = adjoint(mismatch, saved, base, inverse)
         descent = back - earlier
         total, squares = lax.psum(
-            (0.5 * jnp.sum(mismatch * mismatch), jnp.sum(descent * descent)), ("seg", "space")
+            lax.psum((0.5 * jnp.sum(mismatch * mismatch), jnp.sum(descent * descent)), "space"),
+            "seg",
         )
         current = current - total / (squares + EPSILON) * descent
     return (current[None], mismatch[None])

time: 423 us -> 398 us (0.941)
  blocking collectives: 79.3 us -> 55.6 us
    psum x2, blocking collectives: 79.3 us -> 12.9 us  [per_device(): lax.psum((0.5 * jnp.sum(mismatch * mismatch), jnp.sum(descent * descent))...]
    psum x0 -> x2, blocking collectives: none -> 42.7 us  [per_device(): lax.psum(lax.psum((0.5 * jnp.sum(mismatch * mismatch), jnp.sum(descent *...]
  transfers between devices with their start and end apart: 36 -> 36, of which waited for: 33 -> 33; matrix products, arithmetic and copies ran while one was open for 24% -> 25% of each run, Pallas kernels for 0% -> 0%
where the time goes in v1:
time: 398 us; the launch traced here: 395 us
  loops' own time  120 us (30%)
  other arithmetic  84.6 us (21%)
  waiting for transfers between devices  76.5 us (19%)
  blocking collectives  55.6 us (14%)
  local copies, waits for them, and re-layouts  23.5 us (6%)
  starting transfers between devices  16.7 us (4%)
  matrix products  12.8 us (3%)
  between operations  5.26 us (1%)
    another operation x2, loops' own time, inverses(): lax.linalg.tridiagonal_solve(lower[None], centre[None], upper[None], iden...  120 us
    while x62, other arithmetic  77.4 us
    psum x2, blocking collectives, per_device(): lax.psum(lax.psum((0.5 * jnp.sum(mismatch * mismatch), jnp.sum(descent *...  42.7 us
    ppermute x4, waiting for transfers between devices, shifted(): return lax.ppermute(block, axis, route)  33.8 us
    ppermute x16, waiting for transfers between devices, padded_2(): before = lax.ppermute(last, axis, up)  27.8 us
    ppermute x16, waiting for transfers between devices, padded_2(): after = lax.ppermute(initial, axis, down)  14.9 us
    psum x2, blocking collectives, per_device(): lax.psum((0.5 * jnp.sum(mismatch * mismatch), jnp.sum(descent * descent))...  12.9 us
    slice x20, local copies, waits for them, and re-layouts, inverses(): lax.linalg.tridiagonal_solve(lower[None], centre[None], upper[None], iden...  11.7 us
  transfers between devices with their start and end apart: 36, of which 33 were waited for; matrix products, arithmetic and copies ran while one was open for 25% of the time, Pallas kernels for 0%

profile of v1, /device:TPU:0, one launch (start us, length us, event | category | flops | bytes accessed | tf_op | source)
XLA Modules:
  0.0 395.2 jit_solution(7154879211111134166)
XLA Ops:
  0.6 1.0 copy.69
  1.7 2.5 collective-permute-start
  5.8 169.7 %while.32 = (s32[]{:T(128)}, f32[1]{0:T(128)}, f32[1,65]{1,0:T(1,128)S(1)}, f32[2,32,1]{1,2,0:T(1,128)S(1)}, f32[2,32,1,65]{3,1,2,0:T(8,128)S(1)}, /*index=5*/f3...) while((s32[]{:T(128)}, f32[1]{0:T(128)}, ...), condition=%wide.region_1.2_spmd, body=%wide.region_0.1_spmd.sunk | while | flops 6369 | bytes 103045 | solution.py:42
  7.9 0.7 fusion.724
  8.6 0.7 fusion.726
  10.0 0.7 fusion.725
  92.8 0.7 fusion.724
  93.5 0.7 fusion.726
  94.9 0.7 fusion.725
  175.5 43.9 %while.33 = (s32[]{:T(128)}, f32[1,65]{1,0:T(1,128)S(1)}, f32[2,32,1,65]{3,1,2,0:T(8,128)S(1)}, f32[2,32,1,65]{3,2,1,0:T(1,128)S(1)}, f32[2,32,1]{1,2,0:T(1,128)...) while((s32[]{:T(128)}, f32[1,65]{1,0:T(1,128)S(1)}, ...), condition=%wide.region_3.4_spmd, body=%wide.region_2.3_spmd.sunk | while | flops 4193 | bytes 91485 | solution.py:42
  176.2 0.7 fusion.729
  176.9 19.5 %constant_dynamic-update-slice_fusion.168 = (f32[32,1,65]{2,1,0:T(1,128)S(1)}, f32[1,65]{1,0:T(1,128)S(1)}, f32[1,65]{1,0:T(1,128)S(1)}, f32[1,65]{1,0:T(1,128)S...) fusion(f32[]{:T(128)} %bitcast.1400, ...), kind=kLoop, calls=%fused_computation.196.clone.1 | loop fusion | flops 4029 | bytes 24956 | tf_op jit(solution)/shard_map/vmap()/while
  198.2 0.7 fusion.729
  198.9 19.5 %constant_dynamic-update-slice_fusion.168 = (f32[32,1,65]{2,1,0:T(1,128)S(1)}, f32[1,65]{1,0:T(1,128)S(1)}, f32[1,65]{1,0:T(1,128)S(1)}, f32[1,65]{1,0:T(1,128)S...) fusion(f32[]{:T(128)} %bitcast.1400, ...), kind=kLoop, calls=%fused_computation.196.clone.1 | loop fusion | flops 4029 | bytes 24956 | tf_op jit(solution)/shard_map/vmap()/while
  220.3 1.8 collective-permute-start.2
  222.2 1.7 collective-permute-done.2
  223.9 1.6 collective-permute-done.3
  227.2 1.5 collective-permute-done.4
  228.7 1.7 collective-permute-done.5
  232.0 1.3 collective-permute-done.6
  233.3 1.9 collective-permute-done.7
  235.2 1.5 convolution_bitcast_fusion.12
  236.7 1.5 collective-permute-start.8
  238.2 8.9 %collective-permute-done.8 = f32[8,65,128]{2,1,0:T(8,128)S(1)} collective-permute-done((f32[8,65,128]{2,1,0:T(8,128)S(1)}, f32[8,65,128]{2,1,0:T(8,128)S(1)}, u32[]{:S(2)}, u32[]{:S(2)}) %collective-permute-start.8) | collective-permute-done | bytes 266272 | tf_op jit(solution)/shard_map/ppermute | solution.py:31
  247.2 1.8 collective-permute-start.9
  248.9 5.0 %collective-permute-done.9 = f32[8,65,128]{2,1,0:T(8,128)S(1)} collective-permute-done((f32[8,65,128]{2,1,0:T(8,128)S(1)}, f32[8,65,128]{2,1,0:T(8,128)S(1)}, u32[]{:S(2)}, u32[]{:S(2)}) %collective-permute-start.9) | collective-permute-done | bytes 266272 | tf_op jit(solution)/shard_map/ppermute | solution.py:31
  254.6 0.9 fusion.694
  256.1 1.6 collective-permute-start.10
  257.7 0.7 multiply_reduce_fusion.3
  259.7 2.2 collective-permute-done.11
  261.9 1.7 add_multiply_fusion.5
  264.5 0.8 collective-permute-done.12
  265.3 2.0 collective-permute-done.13
  268.9 0.8 collective-permute-done.14
  269.7 2.0 collective-permute-done.15
  273.2 0.8 collective-permute-done.16
  274.1 2.0 collective-permute-done.17
  276.0 0.9 multiply_reduce_fusion.2
  276.9 6.4 %all-reduce.3 = (f32[]{:T(128)}, f32[]{:T(128)}) all-reduce(f32[]{:T(128)S(6)} %mul.1494, f32[]{:T(128)} %get-tuple-element.308), channel_id=1, replica_groups=mesh['seg'=8,'space'=4] {'space'}, use_global_device_ids=true, to_apply=%region_5.6 | all-reduce | flops 2 | bytes 16 | tf_op jit(solution)/shard_map/psum | solution.py:104
  283.3 22.0 %all-reduce.1 = (f32[]{:T(128)}, f32[]{:T(128)}) all-reduce(f32[]{:T(128)} %get-tuple-element.210, f32[]{:T(128)} %get-tuple-element.211), channel_id=1, replica_groups=mesh['seg'=8,'space'=4] {'seg'}, use_global_device_ids=true, to_apply=%region_6.7 | all-reduce | flops 2 | bytes 16 | tf_op jit(solution)/shard_map/psum | solution.py:103
  307.6 1.0 collective-permute-done.18
  308.6 2.3 collective-permute-done.19
  312.5 1.0 collective-permute-done.20
  313.4 2.0 collective-permute-done.21
  317.0 1.0 collective-permute-done.22
  318.0 2.0 collective-permute-done.23
  321.5 1.0 collective-permute-done.24
  322.5 2.0 collective-permute-done.25
  325.2 11.7 %collective-permute-done.26 = f32[8,65,128]{2,1,0:T(8,128)S(1)} collective-permute-done((f32[8,65,128]{2,1,0:T(8,128)S(1)}, f32[8,65,128]{2,1,0:T(8,128)S(1)}, u32[]{:S(2)}, u32[]{:S(2)}) %collective-permute-start.26) | collective-permute-done | bytes 266272 | tf_op jit(solution)/shard_map/ppermute | solution.py:31
  337.1 8.2 %collective-permute-done.27 = f32[8,65,128]{2,1,0:T(8,128)S(1)} collective-permute-done((f32[8,65,128]{2,1,0:T(8,128)S(1)}, f32[8,65,128]{2,1,0:T(8,128)S(1)}, u32[]{:S(2)}, u32[]{:S(2)}) %collective-permute-start.27) | collective-permute-done | bytes 266272 | tf_op jit(solution)/shard_map/ppermute | solution.py:31
  345.9 0.9 fusion.670
  349.2 0.8 copy.22
  350.0 1.1 collective-permute-done.29
  351.1 1.4 add_multiply_fusion.1
  353.4 1.2 collective-permute-done.30
  354.6 1.7 collective-permute-done.31
  357.8 1.2 collective-permute-done.32
  359.0 1.7 collective-permute-done.33
  362.3 1.1 collective-permute-done.34
  363.3 1.7 collective-permute-done.35
  365.1 0.9 multiply_reduce_fusion
  366.0 6.5 %all-reduce.2 = (f32[]{:T(128)}, f32[]{:T(128)}) all-reduce(f32[]{:T(128)S(6)} %mul.1544, f32[]{:T(128)} %get-tuple-element.306), channel_id=1, replica_groups=mesh['seg'=8,'space'=4] {'space'}, use_global_device_ids=true, to_apply=%region_11.12 | all-reduce | flops 2 | bytes 16 | tf_op jit(solution)/shard_map/psum | solution.py:104
  372.5 20.7 %all-reduce = (f32[]{:T(128)}, f32[]{:T(128)}) all-reduce(f32[]{:T(128)} %get-tuple-element.208, f32[]{:T(128)} %get-tuple-element.209), channel_id=1, replica_groups=mesh['seg'=8,'space'=4] {'seg'}, use_global_device_ids=true, to_apply=%region_12.13 | all-reduce | flops 2 | bytes 16 | tf_op jit(solution)/shard_map/psum | solution.py:103
  394.4 0.8 copy.21
  (303 shorter events, 72.7 us)
Async XLA Ops:
  1.7 217.7 %collective-permute-start = (f32[1,65,128]{2,1,0:T(8,128)S(1)}, f32[1,65,128]{2,1,0:T(8,128)S(1)}, u32[]{:S(2)}, u32[]{:S(2)}) collective-permute-start(f32[1,65,128]{2,1,0:T(8,128)S(1)} %get-tuple-element.530), channel_id=1, source_target_pairs={{1,0},{2,1},{3,2},{0,3},{5,4},{6,5},{7,6},{4,7},{9,8},{10,9},{11,1... | collective-permute-start | bytes 99848 | tf_op jit(solution)/shard_map/ppermute | solution.py:23
  4.1 215.3 %collective-permute-start.1 = (f32[1,65,128]{2,1,0:T(8,128)S(1)}, f32[1,65,128]{2,1,0:T(8,128)S(1)}, u32[]{:S(2)}, u32[]{:S(2)}) collective-permute-start(f32[1,65,128]{2,1,0:T(8,128)S(1)} %get-tuple-element.531), channel_id=1, source_target_pairs={{0,1},{1,2},{2,3},{3,0},{4,5},{5,6},{6,7},{7,4},{8,9},{9,10},{10,1... | collective-permute-start | bytes 99848 | tf_op jit(solution)/shard_map/ppermute | solution.py:22
  4.3 0.7 copy-start.17
  175.5 44.0 %copy-start = (f32[8,65,128]{2,0,1:T(8,128)S(1)}, f32[8,65,128]{2,0,1:T(8,128)}, u32[]{:S(2)}) copy-start(f32[8,65,128]{2,0,1:T(8,128)} %param.8) | copy-start | bytes 798724
  219.4 0.7 copy-start.3
  219.4 0.7 copy-start.5
  220.3 3.6 collective-permute-start.2
  222.1 3.4 collective-permute-start.3
  223.9 2.3 copy-start.7
  225.5 0.7 copy-start.9
  226.3 2.4 collective-permute-start.4
  227.0 3.4 collective-permute-start.5
  228.7 2.4 copy-start.11
  230.4 0.7 copy-start.13
  231.3 2.0 collective-permute-start.6
  231.7 3.5 collective-permute-start.7
  235.2 11.9 %copy-start.1 = (f32[1,8,65,128]{3,1,2,0:T(8,128)S(1)}, f32[1,8,65,128]{3,1,2,0:T(8,128)}, u32[]{:S(2)}) copy-start(f32[1,8,65,128]{3,1,2,0:T(8,128)} %param.7) | copy-start | bytes 798724
  236.7 10.4 %collective-permute-start.8 = (f32[8,65,128]{2,1,0:T(8,128)S(1)}, f32[8,65,128]{2,1,0:T(8,128)S(1)}, u32[]{:S(2)}, u32[]{:S(2)}) collective-permute-start(f32[8,65,128]{2,1,0:T(8,128)S(1)} %convolution_bitcast_fusion.12), channel_id=1, source_target_pairs={{28,0},{0,4},{4,8},{8,12},{12,16},{16,20},{20,24},{24,28},{29,1},{... | collective-permute-start | bytes 798728 | tf_op jit(solution)/shard_map/ppermute | solution.py:31
  247.2 6.8 %collective-permute-start.9 = (f32[8,65,128]{2,1,0:T(8,128)S(1)}, f32[8,65,128]{2,1,0:T(8,128)S(1)}, u32[]{:S(2)}, u32[]{:S(2)}) collective-permute-start(f32[8,65,128]{2,1,0:T(8,128)S(1)} %bitcast_subtract_fusion), channel_id=1, source_target_pairs={{4,0},{8,4},{12,8},{16,12},{20,16},{24,20},{28,24},{0,28},{5,1},{9... | collective-permute-start | bytes 798728 | tf_op jit(solution)/shard_map/ppermute | solution.py:31
  256.1 3.6 collective-permute-start.10
  257.7 4.2 %collective-permute-start.11 = (f32[1,65,128]{2,1,0:T(8,128)}, f32[1,65,128]{2,1,0:T(8,128)}, u32[]{:S(2)}, u32[]{:S(2)}) collective-permute-start(f32[1,65,128]{2,1,0:T(8,128)} %get-tuple-element.511), channel_id=1, source_target_pairs={{0,1},{1,2},{2,3},{3,0},{4,5},{5,6},{6,7},{7,4},{8,9},{9,10},{10,1... | collective-permute-start | bytes 99848 | tf_op jit(solution)/shard_map/ppermute | solution.py:22
  263.6 1.7 collective-permute-start.12
  263.7 3.6 collective-permute-start.13
  264.4 3.0 copy-start.12
  264.4 3.0 copy-start.14
  268.0 1.7 collective-permute-start.14
  268.1 3.6 collective-permute-start.15
  268.7 2.9 copy-start.8
  268.7 2.9 copy-start.10
  272.4 1.7 collective-permute-start.16
  272.4 3.6 collective-permute-start.17
  273.1 2.9 copy-start.4
  273.1 2.9 copy-start.6
  306.9 1.7 collective-permute-start.18
  307.0 3.9 collective-permute-start.19
  311.8 1.7 collective-permute-start.20
  311.8 3.7 collective-permute-start.21
  316.3 1.7 collective-permute-start.22
  316.4 3.6 collective-permute-start.23
  320.8 1.7 collective-permute-start.24
  320.9 3.6 collective-permute-start.25
  324.5 0.7 copy-start.15
  325.2 11.8 %collective-permute-start.26 = (f32[8,65,128]{2,1,0:T(8,128)S(1)}, f32[8,65,128]{2,1,0:T(8,128)S(1)}, u32[]{:S(2)}, u32[]{:S(2)}) collective-permute-start(f32[8,65,128]{2,1,0:T(8,128)S(1)} %convolution_bitcast_fusion.4), channel_id=1, source_target_pairs={{28,0},{0,4},{4,8},{8,12},{12,16},{16,20},{20,24},{24,28},{29,1},{... | collective-permute-start | bytes 798728 | tf_op jit(solution)/shard_map/ppermute | solution.py:31
  337.0 8.3 %collective-permute-start.27 = (f32[8,65,128]{2,1,0:T(8,128)S(1)}, f32[8,65,128]{2,1,0:T(8,128)S(1)}, u32[]{:S(2)}, u32[]{:S(2)}) collective-permute-start(f32[8,65,128]{2,1,0:T(8,128)S(1)} %sub.738), channel_id=1, source_target_pairs={{4,0},{8,4},{12,8},{16,12},{20,16},{24,20},{28,24},{0,28},{5,1},{9... | collective-permute-start | bytes 798728 | tf_op jit(solution)/shard_map/ppermute | solution.py:31
  347.4 2.6 collective-permute-start.28
  347.4 3.7 collective-permute-start.29
  349.2 1.9 copy-start.2
  349.2 1.9 copy-start.16
  352.5 2.1 collective-permute-start.30
  352.9 3.4 collective-permute-start.31
  357.0 2.0 collective-permute-start.32
  357.4 3.4 collective-permute-start.33
  361.4 1.9 collective-permute-start.34
  361.7 3.4 collective-permute-start.35
